TPU v7x, 32 devices: a whole 2x2x4 slice. The times are simulated.
32 devices in a mesh: dp: 8 (over y, x, core), mp: 4 (over z).
Axes of the slice: x: 2, y: 2, z: 4, core: 2. Of those that a mesh axis runs over, the one named last changes fastest.
Arguments:
- inputs: bfloat16 [16, 1024, 1280], P('dp', 'mp'), may hold values from -6 to 6
- cotangent: bfloat16 [16, 1024, 1280], P('dp', 'mp'), may hold values from -6 to 6
- gene_counts: int32 [16], P('dp'), may hold values from 200 to 1023, as said below
- step_count: int32 [1], replicated, may hold values from 2 to 20
- norm_params: float32 [4, 1280], P(None, ('dp', 'mp')), may hold values from -0.3 to 1.4, as said below
- norm_first: float32 [4, 1280], P(None, ('dp', 'mp')), may hold values from -80 to 80
- norm_second: float32 [4, 1280], P(None, ('dp', 'mp')), may hold values from 425.984 to 6881.28
- attend_weight: float32 [3, 1280, 1280], P(None, 'dp', 'mp'), may hold values from -0.15625 to 0.15625
- attend_first: float32 [3, 1280, 1280], P(None, 'dp', 'mp'), may hold values from -80 to 80
- attend_second: float32 [3, 1280, 1280], P(None, 'dp', 'mp'), may hold values from 425.984 to 6881.28
- output_weight: float32 [1280, 1280], P('mp', 'dp'), may hold values from -4 to 4
- output_first: float32 [1280, 1280], P('mp', 'dp'), may hold values from -4 to 4
- output_second: float32 [1280, 1280], P('mp', 'dp'), may hold values from 0.8 to 13.44
- expand_weight: float32 [1280, 5120], P('dp', 'mp'), may hold values from -0.15625 to 0.15625
- expand_first: float32 [1280, 5120], P('dp', 'mp'), may hold values from -32 to 32
- expand_second: float32 [1280, 5120], P('dp', 'mp'), may hold values from 68.8128 to 1097.728
- reduce_weight: float32 [5120, 1280], P('mp', 'dp'), may hold values from -0.078125 to 0.078125
- reduce_first: float32 [5120, 1280], P('mp', 'dp'), may hold values from -48 to 48
- reduce_second: float32 [5120, 1280], P('mp', 'dp'), may hold values from 155.648 to 2457.6
Outputs:
- outputs: float32 [16, 1024, 1280], P('dp', 'mp')
- input_grad: float32 [16, 1024, 1280], P('dp', 'mp')
- norm_master: float32 [4, 1280], P(None, ('dp', 'mp'))
- norm_momentum: float32 [4, 1280], P(None, ('dp', 'mp'))
- norm_variance: float32 [2, 1280], P(None, ('dp', 'mp'))
- feed_variance: float32 [2, 1280], P(None, ('dp', 'mp'))
- attend_master: float32 [3, 1280, 1280], P(None, 'dp', 'mp')
- attend_momentum: float32 [3, 1280, 1280], P(None, 'dp', 'mp')
- attend_variance: float32 [3, 1280, 1280], P(None, 'dp', 'mp')
- output_master: float32 [1280, 1280], P('mp', 'dp')
- output_momentum: float32 [1280, 1280], P('mp', 'dp')
- output_variance: float32 [1280, 1280], P('mp', 'dp')
- expand_master: float32 [1280, 5120], P('dp', 'mp')
- expand_momentum: float32 [1280, 5120], P('dp', 'mp')
- expand_variance: float32 [1280, 5120], P('dp', 'mp')
- reduce_master: float32 [5120, 1280], P('mp', 'dp')
- reduce_momentum: float32 [5120, 1280], P('mp', 'dp')
- reduce_variance: float32 [5120, 1280], P('mp', 'dp')
Inputs may be any that keep to these rules, and one draw needn't show every extreme that they name: `gene_counts`: genes of each cell; the cell holds that many tokens plus its CLS token, the rest of its 1024 slots are padding; the largest, 1023, occurs in every draw. `norm_params`: rows 0 and 2 are gains, rows 1 and 3 shifts.
All inputs are finite; a program needn't handle non-finite values.
Results may differ from a plain program's by a relative error of at most 0.012.
Values may be sent and summed in bfloat16 or wider, within the bound.
A program may use at most 256 MiB of HBM per device.

v0:
```python
import functools

import jax
import jax.numpy as jnp
from jax import lax
from jax.experimental import pallas as pl
from jax.experimental.pallas import tpu as pltpu
from jax.sharding import PartitionSpec as P

D = 1280
HEAD_DIM = 64
FF = 5120
SEQ = 1024

eps_norm = 1e-05
masked_score = -1e30
beta_one = 0.9
beta_two = 0.95
eps_adam = 1e-08
decay_rate = 0.1
norm_rate = 0.6

F32 = jnp.float32
BF16 = jnp.bfloat16
AXES = ("dp", "mp")


def exact_gelu(values):
    return jax.nn.gelu(values, approximate=False)


def mm(left, right, dims):
    return lax.dot_general(left, right, (dims, ((), ())), preferred_element_type=F32)


def mm_nn(left, right):
    return mm(left, right, ((1,), (0,)))


def mm_nt(left, right):
    return mm(left, right, ((1,), (1,)))


def mm_tn(left, right):
    return mm(left, right, ((0,), (0,)))


def normalize(token_rows, norm_gain, norm_shift):
    mean_row = jnp.mean(token_rows, axis=-1, keepdims=True)
    centred = token_rows - mean_row
    inv_std = lax.rsqrt(jnp.mean(centred * centred, axis=-1, keepdims=True) + eps_norm)
    scaled = centred * inv_std
    return (scaled * norm_gain + norm_shift, scaled, inv_std)


def normalize_back(grad_out, scaled, inv_std, norm_gain):
    grad_scaled = grad_out * norm_gain
    centre_part = jnp.mean(grad_scaled, axis=-1, keepdims=True)
    along_part = scaled * jnp.mean(grad_scaled * scaled, axis=-1, keepdims=True)
    grad_in = inv_std * (grad_scaled - centre_part - along_part)
    return (grad_in, jnp.sum(grad_out * scaled, axis=0), jnp.sum(grad_out, axis=0))


def adam_step(weight, first_moment, second_moment, gradient, rate, decay, step_number):
    first_new = beta_one * first_moment + (1.0 - beta_one) * gradient
    second_new = beta_two * second_moment + (1.0 - beta_two) * gradient * gradient
    corr_one = 1.0 - jnp.power(beta_one, step_number)
    corr_two = 1.0 - jnp.power(beta_two, step_number)
    update = first_new / corr_one / (jnp.sqrt(second_new / corr_two) + eps_adam)
    return (weight - rate * (update + decay * weight), first_new, second_new)


def attend_kernel(heads, block, bias_ref, q_ref, kv_ref, ctx_ref, lse_ref):
    width = heads * HEAD_DIM
    bias = bias_ref[...]
    for h in range(heads):
        lo = h * HEAD_DIM
        q = q_ref[0, :, lo : lo + HEAD_DIM] * jnp.asarray(HEAD_DIM**-0.5, BF16)
        k = kv_ref[0, :, width + lo : width + lo + HEAD_DIM]
        v = kv_ref[0, :, 2 * width + lo : 2 * width + lo + HEAD_DIM]
        s = mm_nt(q, k) + bias
        top = jnp.max(s, axis=-1, keepdims=True)
        e = jnp.exp(s - top)
        total = jnp.sum(e, axis=-1, keepdims=True)
        ctx = mm_nn(e.astype(BF16), v) / total
        ctx_ref[0, :, lo : lo + HEAD_DIM] = ctx.astype(BF16)
        lse_ref[0, :, h : h + 1] = top + jnp.log(total)


def attend(qkv, bias, heads):
    chunks, seq, _ = qkv.shape
    block = min(256, seq)
    width = heads * HEAD_DIM
    return pl.pallas_call(
        functools.partial(attend_kernel, heads, block),
        grid=(chunks, seq // block),
        in_specs=[
            pl.BlockSpec((1, seq), lambda i, j: (0, 0)),
            pl.BlockSpec((1, block, 3 * width), lambda i, j: (i, j, 0)),
            pl.BlockSpec((1, seq, 3 * width), lambda i, j: (i, 0, 0)),
        ],
        out_specs=[
            pl.BlockSpec((1, block, width), lambda i, j: (i, j, 0)),
            pl.BlockSpec((1, block, 8), lambda i, j: (i, j, 0)),
        ],
        out_shape=[
            jax.ShapeDtypeStruct((chunks, seq, width), BF16),
            jax.ShapeDtypeStruct((chunks, seq, 8), F32),
        ],
        cost_estimate=pl.CostEstimate(
            flops=16 * chunks * heads * seq * seq * HEAD_DIM,
            bytes_accessed=8 * chunks * seq * width,
            transcendentals=chunks * heads * seq * seq,
        ),
        name="attend",
    )(bias, qkv, qkv)


def attend_back_kernel(heads, bias_ref, q_ref, g_ref, o_ref, lse_ref, kv_ref, gq_ref, gkv_ref, acc_ref):
    width = heads * HEAD_DIM
    step = pl.program_id(1)
    scale = HEAD_DIM**-0.5

    @pl.when(step == 0)
    def _():
        acc_ref[...] = jnp.zeros_like(acc_ref)

    bias = bias_ref[...]
    lse_rows = lse_ref[0].T
    for h in range(heads):
        lo = h * HEAD_DIM
        q = q_ref[0, :, lo : lo + HEAD_DIM] * jnp.asarray(scale, BF16)
        g = g_ref[0, :, lo : lo + HEAD_DIM]
        o = o_ref[0, :, lo : lo + HEAD_DIM]
        k = kv_ref[0, :, width + lo : width + lo + HEAD_DIM]
        v = kv_ref[0, :, 2 * width + lo : 2 * width + lo + HEAD_DIM]
        delta = jnp.sum(g.astype(F32) * o.astype(F32), axis=-1, keepdims=True).T
        st = mm_nt(k, q) + bias
        pt = jnp.exp(st - lse_rows[h : h + 1, :])
        gpt = mm_nt(v, g)
        gst = (pt * (gpt - delta)).astype(BF16)
        acc_ref[:, width + lo : width + lo + HEAD_DIM] += mm_nn(pt.astype(BF16), g)
        acc_ref[:, lo : lo + HEAD_DIM] += mm_nn(gst, q)
        gq_ref[0, :, lo : lo + HEAD_DIM] = (mm_tn(gst, k) * scale).astype(BF16)

    @pl.when(step == pl.num_programs(1) - 1)
    def _():
        gkv_ref[0] = acc_ref[...].astype(BF16)


def attend_back(qkv, grad_ctx, ctx, lse, bias_col, heads):
    chunks, seq, _ = qkv.shape
    block = min(256, seq)
    width = heads * HEAD_DIM
    return pl.pallas_call(
        functools.partial(attend_back_kernel, heads),
        grid=(chunks, seq // block),
        in_specs=[
            pl.BlockSpec((seq, 1), lambda i, j: (0, 0)),
            pl.BlockSpec((1, block, 3 * width), lambda i, j: (i, j, 0)),
            pl.BlockSpec((1, block, width), lambda i, j: (i, j, 0)),
            pl.BlockSpec((1, block, width), lambda i, j: (i, j, 0)),
            pl.BlockSpec((1, block, 8), lambda i, j: (i, j, 0)),
            pl.BlockSpec((1, seq, 3 * width), lambda i, j: (i, 0, 0)),
        ],
        out_specs=[
            pl.BlockSpec((1, block, width), lambda i, j: (i, j, 0)),
            pl.BlockSpec((1, seq, 2 * width), lambda i, j: (i, 0, 0)),
        ],
        out_shape=[
            jax.ShapeDtypeStruct((chunks, seq, width), BF16),
            jax.ShapeDtypeStruct((chunks, seq, 2 * width), BF16),
        ],
        scratch_shapes=[pltpu.VMEM((seq, 2 * width), F32)],
        cost_estimate=pl.CostEstimate(
            flops=40 * chunks * heads * seq * seq * HEAD_DIM,
            bytes_accessed=20 * chunks * seq * width,
            transcendentals=chunks * heads * seq * seq,
        ),
        name="attend_back",
    )(bias_col, qkv, grad_ctx, ctx, lse, qkv)


class Routes:
    def __init__(self, dp_size, mp_size):
        self.dp, self.mp = dp_size, mp_size
        self.bits = (dp_size // 2).bit_length() - 1
        self.mp_bits = mp_size.bit_length() - 1

    def _pairs(self, target):
        pairs = []
        for d in range(self.dp):
            for m in range(self.mp):
                dest = target(d // 2, d % 2, m)
                pairs.append((d * self.mp + m, (dest[0] * 2 + dest[1]) * self.mp + dest[2]))
        return pairs

    def send(self, value, target, back=False):
        pairs = self._pairs(target)
        if back:
            pairs = [(b, a) for a, b in pairs]
        return lax.ppermute(value, AXES, pairs)

    def partner(self, value):
        return self.send(value, lambda p, c, m: (p, 1 - c, m))

    def pair_bit(self, value, bit):
        return self.send(value, lambda p, c, m: (p ^ (1 << bit), c, m))

    def mp_bit(self, value, bit):
        return self.send(value, lambda p, c, m: (p, c, m ^ (1 << bit)))

    def cell(self, value, k, back=False):
        return self.send(value, lambda p, c, m: (p, m // 2, 2 * c + ((m % 2) ^ k)), back)

    def shard(self, value, k, back=False):
        return self.send(value, lambda p, c, m: (p, m // 2, m ^ k ^ (2 * c)), back)


def gather_shards(routes, shard):
    got = [routes.shard(shard, k) for k in range(4)]
    chunks = []
    for half in range(2):
        own = jnp.stack([got[half], got[half + 2]])
        order = range(routes.bits) if half else reversed(range(routes.bits))
        pieces = {0: own}
        for bit in order:
            if routes.bits <= 2:
                pieces.update({r | (1 << bit): routes.pair_bit(v, bit) for r, v in list(pieces.items())})
            else:
                keys = sorted(pieces)
                cat = routes.pair_bit(jnp.stack([pieces[r] for r in keys]), bit)
                pieces.update({r | (1 << bit): cat[i] for i, r in enumerate(keys)})
        chunks.append(pieces)
    return chunks


def assemble(pieces, mask):
    count = len(pieces)
    _, rows, width = pieces[0].shape
    full = jnp.zeros((count * 2 * rows, width), pieces[0].dtype)
    for r in range(count):
        for e in range(2):
            full = lax.dynamic_update_slice(full, pieces[r][e], ((((2 * r + e) ^ mask)) * rows, 0))
    return full


def scatter_grads(routes, chunks, mask):
    partial = []
    for half in range(2):
        full = chunks[half]
        count = 1 << routes.bits
        rows = full.shape[0] // (2 * count)
        blocks = full.reshape(2 * count, rows, full.shape[1])
        pieces = {
            r: jnp.stack([lax.dynamic_index_in_dim(blocks, (2 * r + e) ^ mask, 0, keepdims=False) for e in range(2)])
            for r in range(count)
        }
        order = range(routes.bits) if not half else reversed(range(routes.bits))
        for bit in order:
            keys = sorted(r for r in pieces if not r & (1 << bit))
            sent = routes.pair_bit(jnp.stack([pieces[r | (1 << bit)] for r in keys]), bit)
            pieces = {
                r: (pieces[r].astype(F32) + sent[i].astype(F32)).astype(BF16) for i, r in enumerate(keys)
            }
        partial.append(pieces[0])
    total = None
    for k in range(4):
        got = routes.shard(partial[k % 2][k // 2], k, back=True).astype(F32)
        total = got if total is None else total + got
    return total


MESH = pl.DeviceIdType.MESH


class Here:
    def __init__(self):
        self.d, self.m = lax.axis_index("dp"), lax.axis_index("mp")
        self.c = self.d % 2
        self.pair = self.d - self.c
        self.x = (self.d // 2) % 2
        self.y = self.d // 4
        self.t = self.m // 2
        self.b = self.m % 2
        self.over_x = {"dp": self.d + 2 - 4 * self.x, "mp": self.m}
        self.over_y = {"dp": self.d + 4 - 8 * self.y, "mp": self.m}
        self.partner = {"dp": self.d + 1 - 2 * self.c, "mp": self.m}
        self.home = self.t == self.c

    def at(self, core, m):
        return {"dp": self.pair + core, "mp": m}


def remote(src, dst, ssem, rsem, dev):
    return pltpu.make_async_remote_copy(
        src_ref=src, dst_ref=dst, send_sem=ssem, recv_sem=rsem, device_id=dev, device_id_type=MESH
    )


def arrived(dst, rsem, dev):
    remote(dst, dst, rsem, rsem, dev).wait_recv()


class Maybe:
    def __init__(self, src, dst, ssem, rsem, dev, own):
        self.args, self.dev, self.ssem, self.own = (src, dst), dev, ssem, own
        self.rsem = rsem

    def far(self):
        return remote(*self.args, self.ssem, self.rsem, self.dev)

    def start(self):
        pl.when(self.own)(lambda: pltpu.make_async_copy(*self.args, self.rsem).start())
        pl.when(jnp.logical_not(self.own))(lambda: self.far().start())

    def wait_send(self):
        pl.when(jnp.logical_not(self.own))(lambda: self.far().wait_send())


def greet(here):
    barrier = pltpu.get_barrier_semaphore()

    def tell(dev):
        pl.semaphore_signal(barrier, inc=1, device_id=dev, device_id_type=MESH)

    for core in range(2):
        for m in range(4):
            other = jnp.logical_or(here.c != core, here.m != m)
            pl.when(other)(functools.partial(tell, here.at(core, m)))
    tell(here.over_x)
    tell(here.over_y)
    pl.semaphore_wait(barrier, 9)


class Gather:
    def __init__(self, here, shard, full, sems, relayed):
        self.relayed = relayed
        (self.send_z, self.got_z, self.send_f, self.send_x, self.send_y, self.got_x, self.got_y, self.send_r, self.got_r) = sems
        self.here, self.shard, self.full = here, shard, full
        self.rows = shard.shape[0]
        self.first = jnp.where(here.m > 2 * here.c, 1, 0)

    @staticmethod
    def scratch():
        dma = pltpu.SemaphoreType.DMA
        return [dma((5,))] + [dma((2, 2))] * 8

    def plane(self, i):
        return (self.first + i) % 2

    def block(self, i, dp):
        return self.full.at[self.plane(i), pl.ds(dp * self.rows, self.rows), :]

    def z_copies(self):
        h = self.here
        dst = self.full.at[h.b, pl.ds(h.d * self.rows, self.rows), :]
        got = self.got_z.at[h.b, h.c]
        if self.relayed:
            far = [(h.m < 3, (h.m + 1) % 4), (h.m > 0, (h.m + 3) % 4)]
        else:
            far = [(h.m != m, m) for m in range(4)]
        copies = [
            (there, remote(self.shard, dst, self.send_z.at[n], got, h.at(h.t, m))) for n, (there, m) in enumerate(far)
        ]
        return Maybe(self.shard, dst, self.send_z.at[4], got, h.at(h.t, h.m), h.home), copies

    def start_near(self):
        self.z_copies()[0].start()

    def start_far(self):
        for there, copy in self.z_copies()[1]:
            pl.when(there)(copy.start)

    def onward(self, i, e):
        h = self.here
        source = 2 * h.c + self.plane(i)
        up = source < h.m
        there = jnp.logical_or(jnp.logical_and(up, h.m < 3), jnp.logical_and(source > h.m, h.m > 0))
        ref = self.block(i, h.pair + e)
        target = (h.m + 3 - 2 * up.astype(jnp.int32)) % 4
        return there, remote(ref, ref, self.send_f.at[i, e], self.got_z.at[self.plane(i), e], h.at(h.c, target))

    def own_copies(self, i, e):
        h = self.here
        ref = self.block(i, h.pair + e)
        return (
            remote(ref, ref, self.send_x.at[i, e], self.got_x.at[i, e], h.over_x),
            remote(ref, ref, self.send_y.at[i, e], self.got_y.at[i, e], h.over_y),
        )

    def spread(self, i):
        h = self.here
        for e in range(2):
            arrived(self.block(i, h.pair + e), self.got_z.at[self.plane(i), e], h.partner)
            if self.relayed:
                there, copy = self.onward(i, e)
                pl.when(there)(copy.start)
            for copy in self.own_copies(i, e):
                copy.start()

    def relay_copy(self, i, e):
        h = self.here
        if i == 0:
            ref, dev = self.block(i, h.over_y["dp"] - h.c + e), h.over_x
        else:
            ref, dev = self.block(i, h.over_x["dp"] - h.c + e), h.over_y
        return remote(ref, ref, self.send_r.at[i, e], self.got_r.at[i, e], dev)

    def relay(self, i):
        h = self.here
        for e in range(2):
            if i == 0:
                arrived(self.block(i, h.over_y["dp"] - h.c + e), self.got_y.at[i, e], h.over_y)
            else:
                arrived(self.block(i, h.over_x["dp"] - h.c + e), self.got_x.at[i, e], h.over_x)
            self.relay_copy(i, e).start()

    def finish(self):
        self.arrive()
        self.sent()

    def arrive(self):
        h = self.here
        diagonal = h.pair + 2 - 4 * h.x + 4 - 8 * h.y
        for i in range(2):
            for e in range(2):
                if i == 0:
                    arrived(self.block(i, h.over_x["dp"] - h.c + e), self.got_x.at[i, e], h.over_x)
                else:
                    arrived(self.block(i, h.over_y["dp"] - h.c + e), self.got_y.at[i, e], h.over_y)
                arrived(self.block(i, diagonal + e), self.got_r.at[i, e], h.over_x)

    def sent(self):
        near, far = self.z_copies()
        near.wait_send()
        for there, copy in far:
            pl.when(there)(copy.wait_send)
        for i in range(2):
            for e in range(2):
                if self.relayed:
                    there, copy = self.onward(i, e)
                    pl.when(there)(copy.wait_send)
                for copy in self.own_copies(i, e):
                    copy.wait_send()
                self.relay_copy(i, e).wait_send()


class ToCell:
    def __init__(self, here, source, rows, send, got):
        self.here, self.source, self.rows, self.send, self.got = here, source, rows, send, got

    def copy(self, s):
        h = self.here
        target = 2 * h.c + s
        own = jnp.logical_and(h.home, h.m == target)
        return Maybe(self.source.at[s], self.rows.at[h.b], self.send.at[s], self.got.at[h.b], h.at(h.t, target), own)

    def start(self):
        for s in range(2):
            self.copy(s).start()

    def wait(self):
        for b in range(2):
            arrived(self.rows.at[b], self.got.at[b], self.here.partner)

    def finish(self):
        for s in range(2):
            self.copy(s).wait_send()


class Norms:
    def __init__(self, here, slot, slots, sems):
        self.here, self.slot, self.slots = here, slot, slots
        self.send_z, self.got_z, self.send, self.got = sems

    @staticmethod
    def scratch():
        dma = pltpu.SemaphoreType.DMA
        return [dma((4,)), dma((4,)), dma((3,)), dma((3,))]

    def span(self, d, count):
        return self.slots.at[pl.ds(d * 4 // count * count, count)]

    def z_copy(self, m):
        h = self.here
        return Maybe(self.slot, self.slots.at[h.d * 4 + h.m], self.send_z.at[m], self.got_z.at[h.m], {"dp": h.d, "mp": m}, h.m == m)

    def copy(self, k):
        h = self.here
        ref = self.span(h.d, 4 << k)
        return remote(ref, ref, self.send.at[k], self.got.at[k], (h.partner, h.over_x, h.over_y)[k])

    def start_z(self):
        for m in range(4):
            self.z_copy(m).start()

    def wait_z(self):
        h = self.here
        for m in range(4):
            arrived(self.slots.at[h.d * 4 + m], self.got_z.at[m], h.partner)

    def start(self, k):
        self.copy(k).start()

    def wait(self, k):
        h = self.here
        dev = (h.partner, h.over_x, h.over_y)[k]
        arrived(self.span(dev["dp"], 4 << k), self.got.at[k], dev)

    def sent(self):
        for m in range(4):
            self.z_copy(m).wait_send()
        for k in range(3):
            self.copy(k).wait_send()


def norm_rows(values, gain, shift):
    mean_row = jnp.mean(values, axis=-1, keepdims=True)
    centred = values - mean_row
    inv_std = lax.rsqrt(jnp.mean(centred * centred, axis=-1, keepdims=True) + eps_norm)
    return centred * inv_std * gain + shift


ANY = pl.BlockSpec(memory_space=pl.ANY)
VMEM = pl.BlockSpec(memory_space=pltpu.VMEM)


def rows_at(start, size):
    return pl.ds(start * size, size)


def exact_gelu_both(u):
    below = 0.5 * (1.0 + lax.erf(u * (0.5**0.5)))
    density = jnp.exp(-0.5 * u * u) * ((2.0 * jnp.pi) ** -0.5)
    return u * below, below + u * density


class Stores:
    def __init__(self, sems):
        self.sems, self.made = sems, []

    def put(self, src, dst):
        copy = pltpu.make_async_copy(src, dst, self.sems.at[len(self.made)])
        copy.start()
        self.made.append((src, dst))

    def finish(self):
        for i, (src, dst) in enumerate(self.made):
            pltpu.make_async_copy(src, dst, self.sems.at[i]).wait()


def attend_rows(bias, qkv_ref, ctx_ref, lse_ref, chunk, start, block, heads):
    width = heads * HEAD_DIM
    spare = qkv_ref.shape[2] - 3 * width
    rows = pl.ds(start, block)
    stats = []
    for h in range(heads):
        lo = spare + h * HEAD_DIM
        q = qkv_ref[chunk, rows, lo : lo + HEAD_DIM] * jnp.asarray(HEAD_DIM**-0.5, BF16)
        k = qkv_ref[chunk, :, width + lo : width + lo + HEAD_DIM]
        v = qkv_ref[chunk, :, 2 * width + lo : 2 * width + lo + HEAD_DIM]
        s = mm_nt(q, k) + bias
        top = jnp.max(s, axis=-1, keepdims=True)
        e = jnp.exp(s - top)
        total = jnp.sum(e, axis=-1, keepdims=True)
        ctx = mm_nn(e.astype(BF16), v) / total
        ctx_ref[chunk, rows, h * HEAD_DIM : (h + 1) * HEAD_DIM] = ctx.astype(BF16)
        stats.append(top + jnp.log(total))
    stats += [jnp.zeros_like(stats[0])] * (8 - heads)
    lse_ref[chunk, :, rows] = jnp.concatenate(stats, axis=1).T


def forward_kernel(heads, *refs):
    (x_ref, gy_ref, shard_a, shard_1, shard_2, slot_ref) = refs[:6]
    (full_a, full_1, full_2, h1_out, qkv_out, ctx_out, lse_out, x_out, x2_out, h2_out, act_out, slope_out, gy_out,
     grad_out, norm_ref, count_ref) = refs[6:22]
    (weight, x_in, gy_in, h1, qkv, ctx, lse, fold_out, fold_in, x2, h2, act, slope, gy, stage, slots) = refs[22:38]
    sems = refs[38:]
    (cell_sems, swap_send, swap_got, load_sem, store_sems, stage_sems) = (
        sems[:4], sems[4], sems[5], sems[6], sems[7], sems[8]
    )
    here = Here()
    half, width = x2.shape
    seq = 2 * half
    quarter = half // 2
    inner = heads * HEAD_DIM
    greet(here)
    per = len(Gather.scratch())
    norms = Norms(here, slot_ref, slots, sems[9 + 3 * per :])
    block_a, block_1, block_2 = (
        Gather(here, shard, full, sems[9 + per * i : 9 + per * (i + 1)], i == 0)
        for i, (shard, full) in enumerate(((shard_a, full_a), (shard_1, full_1), (shard_2, full_2)))
    )
    cell_x = ToCell(here, x_ref, x_in, cell_sems[0], cell_sems[1])
    cell_g = ToCell(here, gy_ref, gy_in, cell_sems[2], cell_sems[3])
    stores = Stores(store_sems)

    def swap(n, src, dst):
        return remote(src, dst, swap_send.at[n], swap_got.at[n], here.partner)

    def load(full):
        copies = [pltpu.make_async_copy(full.at[b], weight.at[b], load_sem.at[b]) for b in range(2)]
        for copy in copies:
            copy.start()
        for copy in copies:
            copy.wait()

    own, other = pl.ds(0, half), pl.ds(half, half)
    away = jnp.logical_not(here.home)
    norms.start_z()
    block_a.start_far()
    for block in (block_a, block_1, block_2):
        block.start_near()
    block_a.spread(0)
    norms.wait_z()
    norms.start(0)
    block_a.relay(0)
    norms.wait(0)
    norms.start(1)
    cell_x.start()
    block_a.spread(1)
    norms.wait(1)
    norms.start(2)
    block_a.relay(1)
    pl.when(here.home)(lambda: block_1.spread(0))
    block_1.start_far()
    norms.wait(2)
    columns = norm_ref.shape[1] // 32
    for n in range(32):
        norm_ref[:, n * columns : (n + 1) * columns] = slots[n, 0:4, 0:columns]
    lanes = lax.broadcasted_iota(jnp.int32, (1, 128), 1)
    count_row = slots[(here.pair + here.t) * 4 + here.m, 4:5, :]
    count = jnp.sum(jnp.where(lanes == here.b, count_row, 0.0), axis=1, keepdims=True)
    count_ref[...] = jnp.broadcast_to(count, count_ref.shape)
    cell_x.wait()

    step = 128
    per_quarter = quarter // step

    @pl.loop(0, half // step)
    def _(i):
        rows = pl.ds(pl.multiple_of((i % per_quarter) * step, step), step)
        h1[pl.ds(pl.multiple_of(i * step, step), step), :] = norm_rows(
            x_in[i // per_quarter, rows, :].astype(F32), norm_ref[0:1, :], norm_ref[1:2, :]
        ).astype(BF16)

    swap_h1 = swap(0, h1.at[own], h1.at[other])
    swap_h1.start()
    stores.put(x_in, x_out)
    pl.when(away)(lambda: block_1.spread(0))
    block_a.arrive()
    pl.when(here.home)(lambda: block_1.relay(0))
    pl.when(here.home)(lambda: block_2.spread(0))
    load(full_a)
    swap_h1.wait_recv()
    stores.put(h1, h1_out)

    first = 4 * inner - qkv.shape[2]

    @pl.loop(0, 2)
    def _(b):
        for n in range(0, qkv.shape[2], 512):
            qkv[b, :, n : n + 512] = mm_nn(h1[...], weight[b, :, first + n : first + n + 512]).astype(BF16)

    stores.put(qkv, qkv_out)
    bias = key_bias(here, count, lax.broadcasted_iota(jnp.int32, (1, seq), 1), half)
    q_block = 256
    per_chunk = seq // q_block

    @pl.loop(0, 2 * per_chunk)
    def _(i):
        pl.when(jnp.logical_and(i == 1, away))(lambda: block_1.relay(0))
        pl.when(i == 4)(lambda: block_1.spread(1))
        pl.when(i == 4)(lambda: block_2.start_far())
        pl.when(jnp.logical_and(i == 5, here.home))(lambda: block_2.relay(0))
        pl.when(i == 7)(lambda: block_1.relay(1))
        attend_rows(
            bias, qkv, ctx, lse, i // per_chunk, pl.multiple_of((i % per_chunk) * q_block, q_block), q_block, heads
        )

    stores.put(ctx, ctx_out)
    stores.put(lse, lse_out)

    def branch_tile(rows, n):
        cols = pl.ds(pl.multiple_of(n * 256, 256), 256)
        return mm_nt(ctx[0, rows, :], weight[0, cols, 0:inner]) + mm_nt(ctx[1, rows, :], weight[1, cols, 0:inner]), cols

    @pl.loop(0, width // 256)
    def _(n):
        part, cols = branch_tile(other, n)
        fold_out[:, cols] = part.astype(BF16)

    swap_fold = swap(1, fold_out, fold_in)
    swap_fold.start()

    @pl.loop(0, width // 256)
    def _(n):
        part, cols = branch_tile(own, n)
        for b in range(2):
            rows = pl.ds(b * quarter, quarter)
            x2[rows, cols] = x_in[b, :, cols].astype(F32) + part[b * quarter : (b + 1) * quarter]

    pl.when(away)(lambda: block_2.spread(0))
    swap_fold.wait_recv()

    @pl.loop(0, half // step)
    def _(i):
        rows = pl.ds(pl.multiple_of(i * step, step), step)
        middle = x2[rows, :] + fold_in[rows, :].astype(F32)
        x2[rows, :] = middle
        h2[rows, :] = norm_rows(middle, norm_ref[2:3, :], norm_ref[3:4, :]).astype(BF16)

    swap_h2 = swap(2, h2.at[own], h2.at[other])
    swap_h2.start()
    stores.put(x2, x2_out)
    cell_g.start()
    block_1.arrive()
    load(full_1)
    swap_h2.wait_recv()
    stores.put(h2, h2_out)
    per_unit = width // 256

    @pl.loop(0, 2 * per_unit)
    def _(i):
        pl.when(jnp.logical_and(i == 0, away))(lambda: block_2.relay(0))
        pl.when(i == 3)(lambda: block_2.spread(1))
        pl.when(i == 9)(lambda: block_2.relay(1))
        b, cols = i // per_unit, pl.ds(pl.multiple_of((i % per_unit) * 256, 256), 256)
        value, grad = exact_gelu_both(mm_nn(h2[...], weight[b, :, cols]))
        act[b, :, cols] = value.astype(BF16)
        slope[b, :, cols] = grad.astype(BF16)

    stores.put(act, act_out)
    stores.put(slope, slope_out)
    cell_g.wait()

    @pl.loop(0, 2)
    def _(b):
        gy[pl.ds(pl.multiple_of(b * quarter, quarter), quarter), :] = gy_in[b]

    swap_gy = swap(3, gy.at[own], gy.at[other])
    swap_gy.start()
    swap_gy.wait_recv()
    stores.put(gy, gy_out)

    def stage_copy(i):
        slot = i % 2
        return pltpu.make_async_copy(
            stage.at[slot], grad_out.at[:, pl.ds(pl.multiple_of(i * 256, 256), 256), :], stage_sems.at[slot]
        )

    @pl.loop(0, width // 256)
    def _(i):
        pl.when(i >= 2)(lambda: stage_copy(i - 2).wait())
        left = gy[:, pl.ds(pl.multiple_of(i * 256, 256), 256)].T
        for b in range(2):
            stage[i % 2, b] = mm_nn(left, act[b]).astype(BF16)
        stage_copy(i).start()

    for i in range(width // 256 - 2, width // 256):
        stage_copy(i).wait()
    block_2.arrive()
    for block in (block_a, block_1, block_2):
        block.sent()
    cell_x.finish()
    cell_g.finish()
    norms.sent()
    for n, (src, dst) in enumerate(((h1.at[own], h1.at[other]), (fold_out, fold_in), (h2.at[own], h2.at[other]), (gy.at[own], gy.at[other]))):
        swap(n, src, dst).wait_send()
    stores.finish()


def key_bias(here, count, index, half):
    position = jnp.where(index < half, here.c * half + index, (1 - here.c) * half + index - half)
    return jnp.where(position.astype(F32) < 1.0 + count, 0.0, masked_score)


def forward(inputs, cotangent, shards, slot, heads, collective):
    cells, quarter, width = inputs.shape
    rows, wide = shards[0].shape
    half, seq, inner = 2 * quarter, 4 * quarter, heads * HEAD_DIM
    part = (3 * inner + 255) // 256 * 256
    dma = pltpu.SemaphoreType.DMA
    full = ((2, 8 * rows, wide), BF16)
    kept = [
        ((seq, width), BF16), ((2, seq, part), BF16), ((2, seq, inner), BF16), ((2, 8, seq), F32),
        ((2, quarter, width), BF16), ((half, width), F32), ((seq, width), BF16), ((2, seq, wide), BF16),
        ((2, seq, wide), BF16), ((seq, width), BF16), ((2, width, wide), BF16),
    ]
    buffers = [
        full, ((2, quarter, width), BF16), ((2, quarter, width), BF16), kept[0], kept[1], kept[2], kept[3],
        ((half, width), BF16), ((half, width), BF16), kept[5], kept[6], kept[7], kept[8], kept[9],
        ((2, 2, 256, wide), BF16), ((32, 8, 128), F32),
    ]
    return pl.pallas_call(
        functools.partial(forward_kernel, heads),
        out_shape=[jax.ShapeDtypeStruct(*s) for s in [full] * 3 + kept + [((4, width), F32), ((8, 128), F32)]],
        in_specs=[VMEM] * 6,
        out_specs=[ANY] * 14 + [VMEM] * 2,
        scratch_shapes=[pltpu.VMEM(*s) for s in buffers]
        + [dma((2,))] * 4 + [dma((4,)), dma((4,)), dma((2,)), dma((10,)), dma((2,))]
        + Gather.scratch() * 3 + Norms.scratch(),
        compiler_params=pltpu.CompilerParams(
            collective_id=collective, has_side_effects=True, vmem_limit_bytes=67043328
        ),
        name="forward",
    )(inputs, cotangent, *shards, slot)


class Reduce:
    def __init__(self, here, grads, bufs, sems):
        self.here, self.grads = here, grads
        self.own, self.one, self.two, self.far, self.last, self.part = bufs
        (self.sem_own, self.send_one, self.got_one, self.send_two, self.got_two, self.send_z, self.got_far, self.got_z) = sems
        self.piece = self.own.shape[2]
        self.before = None
        self.away = jnp.logical_not(here.home)
        self.outer = here.m % 3 == 0

    @staticmethod
    def scratch(rows, width):
        r = rows // 2
        dma = pltpu.SemaphoreType.DMA
        four = pltpu.VMEM((2, 4, r, width), BF16)
        landing = [pltpu.VMEM((2, 2, 4, r, width), BF16), four, four, pltpu.VMEM((3, 2, r, width), BF16)]
        sems = [dma((2, 2, 4)), dma((2, 2, 4)), dma((2, 4)), dma((2, 4)), dma((2, 4)), dma((2, 4)), dma((3, 2))]
        return pltpu.VMEM((2, 2, r, width), BF16), four, landing, sems

    def rows_of(self, role, dp, j):
        return self.grads.at[role, pl.ds(dp * 2 * self.piece + j * self.piece, self.piece), :]

    def pair_at(self, role, n, far):
        h = self.here
        dx, dy = 2 - 4 * h.x, 4 - 8 * h.y
        first, second = (dx, dy) if role == 0 else (dy, dx)
        return h.pair + (first if far else 0) + (second if n == 0 else 0)

    def copy_one(self, role, n, j):
        dev = self.here.over_x if role == 0 else self.here.over_y
        return remote(
            self.rows_of(role, self.pair_at(role, n, True), j), self.one.at[role, n, j],
            self.send_one.at[role, n, j], self.got_one.at[role, n, j], dev,
        )

    def copy_two(self, role, j):
        dev = self.here.over_y if role == 0 else self.here.over_x
        return remote(
            self.one.at[role, 0, j], self.two.at[role, j], self.send_two.at[role, j], self.got_two.at[role, j], dev
        )

    def to_inner(self, role, j):
        h = self.here
        return remote(
            self.part.at[role, j], self.far.at[role, j], self.send_z.at[role, j], self.got_far.at[role, j],
            h.at(h.c, h.m + 1 - 2 * h.b),
        )

    def to_owner(self, role, j):
        h = self.here
        target = 2 * h.c + role
        slot = jnp.where(self.away, 2, (h.m + target) % 2)
        return remote(
            self.part.at[role, j], self.last.at[slot, j % 2], self.send_z.at[role, j], self.got_z.at[slot, j % 2],
            h.at(j // 2, target),
        )

    def mine(self, role, j):
        return jnp.logical_and(self.here.c == j // 2, self.here.m == 2 * self.here.c + role)

    def direct(self, role, j):
        return jnp.logical_and(self.here.home, jnp.logical_not(self.mine(role, j)))

    def start_one(self, j):
        for n in range(2):
            for role in range(2):
                self.copy_one(role, n, j).start()

    def start(self):
        for j in range(3):
            self.start_one(j)
        for role in range(2):
            for n in range(2):
                self.load_piece(role, n, 0).start()

    def load_piece(self, role, n, j):
        return pltpu.make_async_copy(
            self.rows_of(role, self.pair_at(role, n, False), j), self.own.at[role, n], self.sem_own.at[role, n]
        )

    def add_one(self, role, j):
        h = self.here
        for n in range(2):
            self.load_piece(role, n, j).wait()
            arrived(self.one.at[role, n, j], self.got_one.at[role, n, j], h.over_x)
            total = self.own[role, n].astype(F32) + self.one[role, n, j].astype(F32)
            self.one[role, n, j] = total.astype(BF16)
            if n == 0:
                self.copy_two(role, j).start()
            if j < 3:
                self.load_piece(role, n, j + 1).start()

    def add_two(self, role, j):
        arrived(self.two.at[role, j], self.got_two.at[role, j], self.here.over_x)
        total = (self.one[role, 1, j].astype(F32) + self.two[role, j].astype(F32)).astype(BF16)
        if self.before is not None:
            self.before.z_sent(role, j)

        @pl.when(self.mine(role, j))
        def _():
            self.last[0, j % 2] = total

        @pl.when(jnp.logical_not(self.mine(role, j)))
        def _():
            self.part[role, j] = total

        pl.when(self.direct(role, j))(lambda: self.to_owner(role, j).start())
        pl.when(jnp.logical_and(self.away, self.outer))(lambda: self.to_inner(role, j).start())

    def pass_on(self, role, j):
        @pl.when(jnp.logical_and(self.away, jnp.logical_not(self.outer)))
        def _():
            arrived(self.far.at[role, j], self.got_far.at[role, j], self.here.partner)
            total = self.part[role, j].astype(F32) + self.far[role, j].astype(F32)
            self.part[role, j] = total.astype(BF16)
            self.to_owner(role, j).start()

    def step(self, j):
        for role in range(2):
            if j < 4:
                self.add_one(role, j)
        if j == 0:
            self.start_one(3)
        for role in range(2):
            if 1 <= j <= 4:
                self.add_two(role, j - 1)
        for role in range(2):
            if j >= 2:
                self.pass_on(role, j - 2)

    def z_sent(self, role, j):
        inner = jnp.logical_and(self.away, jnp.logical_not(self.outer))
        pl.when(jnp.logical_or(self.direct(role, j), inner))(lambda: self.to_owner(role, j).wait_send())
        pl.when(jnp.logical_and(self.away, self.outer))(lambda: self.to_inner(role, j).wait_send())

    def finish(self, total, out_ref, sem):
        h = self.here
        for s in range(2):
            pl.when(self.away)(functools.partial(arrived, self.last.at[0, s], self.got_z.at[0, s], h.partner))
            for n in range(1, 3):
                arrived(self.last.at[n, s], self.got_z.at[n, s], h.partner)
            rows = self.last[0, s].astype(F32)
            for n in range(1, 3):
                rows = rows + self.last[n, s].astype(F32)
            total[pl.ds(s * self.piece, self.piece), :] = rows
        copy = pltpu.make_async_copy(total, out_ref, sem)
        copy.start()
        for role in range(2):
            for j in range(4):
                for n in range(2):
                    self.copy_one(role, n, j).wait_send()
                self.copy_two(role, j).wait_send()
        copy.wait()


class FromCell:
    def __init__(self, here, rows, landing, send, got):
        self.here, self.rows, self.landing, self.send, self.got = here, rows, landing, send, got

    def copy(self, b):
        h = self.here
        target = 2 * h.c + b
        own = jnp.logical_and(h.home, h.m == target)
        return Maybe(self.rows.at[b], self.landing.at[h.b], self.send.at[b], self.got.at[h.b], h.at(h.t, target), own)

    def start(self):
        for b in range(2):
            self.copy(b).start()

    def sent(self):
        for b in range(2):
            self.copy(b).wait_send()

    def arrive(self):
        for s in range(2):
            arrived(self.landing.at[s], self.got.at[s], self.here.partner)


def norm_rows_back(values, grad_out, gain):
    mean_row = jnp.mean(values, axis=-1, keepdims=True)
    centred = values - mean_row
    inv_std = lax.rsqrt(jnp.mean(centred * centred, axis=-1, keepdims=True) + eps_norm)
    scaled = centred * inv_std
    grad_scaled = grad_out * gain
    centre_part = jnp.mean(grad_scaled, axis=-1, keepdims=True)
    along_part = scaled * jnp.mean(grad_scaled * scaled, axis=-1, keepdims=True)
    grad_in = inv_std * (grad_scaled - centre_part - along_part)
    return grad_in, jnp.sum(grad_out * scaled, axis=0, keepdims=True), jnp.sum(grad_out, axis=0, keepdims=True)


def attend_rows_back(bias, qkv_ref, gctx_ref, ctx_ref, lse_ref, grad_ref, acc_ref, chunk, start, block, heads):
    width = heads * HEAD_DIM
    spare = -3 * width % 256
    half = acc_ref.shape[0]
    rows = pl.ds(start, block)
    scale = HEAD_DIM**-0.5
    for h in range(heads):
        at = slice(h * HEAD_DIM, (h + 1) * HEAD_DIM)
        lo = spare + h * HEAD_DIM
        q = qkv_ref[chunk, rows, lo : lo + HEAD_DIM] * jnp.asarray(scale, BF16)
        k = qkv_ref[chunk, :, width + lo : width + lo + HEAD_DIM]
        v = qkv_ref[chunk, :, 2 * width + lo : 2 * width + lo + HEAD_DIM]
        g = gctx_ref[chunk, rows, at]
        delta = jnp.sum(g.astype(F32) * ctx_ref[chunk, rows, at].astype(F32), axis=-1, keepdims=True).T
        pt = jnp.exp(mm_nt(k, q) + bias - lse_ref[chunk, h : h + 1, rows])
        gst = (pt * (mm_nt(v, g) - delta)).astype(BF16)
        gk = mm_nn(gst, q)
        gv = mm_nn(pt.astype(BF16), g)
        for n, part in enumerate((gk[:half], gk[half:], gv[:half], gv[half:])):
            acc_ref[:, n * width + h * HEAD_DIM : n * width + (h + 1) * HEAD_DIM] += part
        grad_ref[chunk, rows, lo : lo + HEAD_DIM] = (mm_tn(gst, k) * scale).astype(BF16)


def backward_kernel(heads, *refs):
    (norm_ref, count_ref, full_a, full_1, full_2, h1_in, qkv_in, ctx_in, lse_in, x_src, x2_src, h2_in, act_in, slope_in,
     gy_src, grad_2) = refs[:16]
    (out_ref, gx_ref, sum_a, sum_1, sum_2, norm_out, grad_1, grad_a) = refs[16:24]
    (weight, gy, slope, act, h2, x2, fold_out, fold_in, gctx, ctx, lse, acc, stage, own, part) = refs[24:39]
    landings = [refs[39 + 4 * i : 43 + 4 * i] for i in range(3)]
    sums, sums_in = refs[51:53]
    sems = refs[53:]
    send_rows = stage
    (load_sems, swap_send, swap_got, cell_sems, stage_sems, own_sem, total_sem) = (
        sems[:10], sems[10], sems[11], sems[12:16], sems[16], sems[17], sems[18]
    )
    per = 7
    here = Here()
    half, width = x2.shape
    seq, quarter, inner = 2 * half, half // 2, heads * HEAD_DIM
    part_width = (3 * inner + 255) // 256 * 256
    first = 4 * inner - part_width
    spare = part_width - 3 * inner
    greet(here)
    blocks = [
        Reduce(here, grads, (own, *landings[i], part), (own_sem, *sems[19 + per * i : 19 + per * (i + 1)]))
        for i, grads in enumerate((grad_2, grad_1, grad_a))
    ]
    block_2, block_1, block_a = blocks
    own_rows, other_rows = pl.ds(0, half), pl.ds(half, half)

    def load(n, src, dst):
        return pltpu.make_async_copy(src, dst, load_sems[n])

    copies = {
        "w2": load(0, full_2, weight), "gy": load(1, gy_src, gy), "slope": load(2, slope_in, slope),
        "act": load(3, act_in, act), "h2": load(4, h2_in, h2), "x2": load(5, x2_src, x2), "ctx": load(6, ctx_in, ctx),
        "lse": load(7, lse_in, lse),
    }
    block_2.start()
    for copy in copies.values():
        copy.start()

    def fetch(src, dst):
        copy = load(9, src, dst)
        copy.start()
        return copy

    def swap(n, src, dst):
        return remote(src, dst, swap_send.at[n], swap_got.at[n], here.partner)

    def tile(n):
        return pl.ds(pl.multiple_of(n * 256, 256), 256)

    tiles = width // 256
    per_unit = width // 256

    copies["w2"].wait()
    copies["act"].wait()

    @pl.loop(0, tiles)
    def _(n):
        cols = tile(n)
        fold_out[:, cols] = (
            mm_nt(act[0, other_rows, :], weight[0, cols, :]) + mm_nt(act[1, other_rows, :], weight[1, cols, :])
        ).astype(BF16)

    swaps = [(fold_out, fold_in.at[0]), (fold_out, fold_in.at[1]), (h2.at[own_rows], h2.at[other_rows]), (fold_out, fold_in.at[0])]
    swap(0, *swaps[0]).start()

    for name in ("gy", "slope"):
        copies[name].wait()

    @pl.loop(0, 2 * per_unit)
    def _(i):
        pl.when(i == 4)(lambda: block_2.step(0))
        b, cols = i // per_unit, tile(i % per_unit)
        grad = mm_nn(gy[...], weight[b, :, cols])
        slope[b, :, cols] = (grad * slope[b, :, cols].astype(F32)).astype(BF16)

    block_2.step(1)
    copies["h2"].wait()

    def stage_copy(grads, i, b):
        return pltpu.make_async_copy(stage.at[b], grads.at[b, tile(i), :], stage_sems.at[b])

    @pl.loop(0, tiles)
    def _(i):
        left = h2[:, tile(i)].T
        for b in range(2):
            pl.when(i >= 1)(lambda: stage_copy(grad_1, i - 1, b).wait())
            stage[b] = mm_nn(left, slope[b]).astype(BF16)
            stage_copy(grad_1, i, b).start()
        pl.when(i == 1)(lambda: block_2.step(2))

    for b in range(2):
        stage_copy(grad_1, tiles - 1, b).wait()
    block_2.step(3)
    block_1.start()
    copies["x2"].wait()
    swap(0, *swaps[0]).wait_recv()

    @pl.loop(0, tiles)
    def _(n):
        cols = tile(n)
        mine = mm_nt(act[0, own_rows, :], weight[0, cols, :]) + mm_nt(act[1, own_rows, :], weight[1, cols, :])
        mine = (mine + x2[:, cols] + fold_in[0, :, cols].astype(F32)).astype(BF16)
        for b in range(2):
            send_rows[b, :, cols] = mine[b * quarter : (b + 1) * quarter]

    cell_out = FromCell(here, send_rows, out_ref, cell_sems[0], cell_sems[1])
    cell_out.start()
    fetch(full_1, weight).wait()
    fetched = fetch(qkv_in, act.at[:, :, 0:part_width])
    swap(0, *swaps[0]).wait_send()

    @pl.loop(0, tiles)
    def _(n):
        cols = tile(n)
        fold_out[:, cols] = (
            mm_nt(slope[0, other_rows, :], weight[0, cols, :]) + mm_nt(slope[1, other_rows, :], weight[1, cols, :])
        ).astype(BF16)

    swap(1, *swaps[1]).start()

    @pl.loop(0, tiles)
    def _(n):
        cols = tile(n)
        acc[:, cols] = mm_nt(slope[0, own_rows, :], weight[0, cols, :]) + mm_nt(slope[1, own_rows, :], weight[1, cols, :])

    fetched.wait()
    fetched = fetch(full_a, weight)
    swap(1, *swaps[1]).wait_recv()
    step = 128
    sums[0] = jnp.zeros(sums.shape[1:], F32)

    @pl.loop(0, half // step)
    def _(i):
        rows = pl.ds(pl.multiple_of(i * step, step), step)
        grad_in, gain_sum, shift_sum = norm_rows_back(
            x2[rows, :], acc[rows, :] + fold_in[1, rows, :].astype(F32), norm_ref[2:3, :]
        )
        sums[0, 2:3, :] += gain_sum
        sums[0, 3:4, :] += shift_sum
        grad_in = gy[rows, :].astype(F32) + grad_in
        x2[rows, :] = grad_in
        h2[rows, :] = grad_in.astype(BF16)

    swap(2, *swaps[2]).start()
    fetched.wait()
    fetched = fetch(h1_in, gy)
    block_2.step(4)
    block_1.before, block_a.before = block_2, block_1
    copies["ctx"].wait()
    copies["lse"].wait()
    swap(2, *swaps[2]).wait_recv()

    for b in range(2):
        gctx[b] = mm_nn(h2[...], weight[b, :, 0:inner]).astype(BF16)
        slope[b, :, 0:spare] = jnp.zeros((seq, spare), BF16)
    bias = key_bias(here, count_ref[0:1, 0:1], lax.broadcasted_iota(jnp.int32, (seq, 1), 0), half)
    q_block = 256
    per_chunk = seq // q_block

    @pl.loop(0, 2 * per_chunk)
    def _(i):
        b, j = i // per_chunk, i % per_chunk

        @pl.when(j == 0)
        def _():
            acc[...] = jnp.zeros_like(acc)

        attend_rows_back(
            bias, act, gctx, ctx, lse, slope, acc, b, pl.multiple_of(j * q_block, q_block), q_block, heads
        )

        @pl.when(j == per_chunk - 1)
        def _():
            for n in range(4):
                lo = spare + (1 + n // 2) * inner
                slope[b, pl.ds((n % 2) * half, half), lo : lo + inner] = acc[:, n * inner : (n + 1) * inner].astype(BF16)

        pl.when(i == 0)(lambda: block_1.step(0))
        pl.when(i == 1)(lambda: block_2.step(5))
        pl.when(i == 2)(lambda: block_1.step(1))
        pl.when(i == 4)(lambda: block_1.step(2))
        pl.when(i == 6)(lambda: block_1.step(3))

    fetched.wait()

    cell_out.sent()
    cell_out.arrive()

    @pl.loop(0, tiles)
    def _(i):
        left = gy[:, tile(i)].T
        left_out = h2[:, tile(i)].T
        for b in range(2):
            pl.when(i >= 1)(lambda: stage_copy(grad_a, i - 1, b).wait())
            stage[b, :, first:] = mm_nn(left, slope[b, :, 0:part_width]).astype(BF16)
            stage[b, :, 0:inner] = mm_nn(left_out, ctx[b]).astype(BF16)
            stage_copy(grad_a, i, b).start()

    for b in range(2):
        stage_copy(grad_a, tiles - 1, b).wait()
    fetched = fetch(x_src, stage)
    block_a.start()
    block_1.step(4)
    total = acc.at[0 : sum_2.shape[0], :]
    swap(1, *swaps[1]).wait_send()

    @pl.loop(0, tiles)
    def _(n):
        cols = tile(n)
        fold_out[:, cols] = sum(
            mm_nt(slope[b, other_rows, 0:part_width], weight[b, cols, first:]) for b in range(2)
        ).astype(BF16)

    swap(3, *swaps[3]).start()
    block_2.finish(total, sum_2, total_sem)
    block_1.step(5)

    @pl.loop(0, tiles)
    def _(n):
        cols = tile(n)
        acc[:, cols] = sum(mm_nt(slope[b, own_rows, 0:part_width], weight[b, cols, first:]) for b in range(2))

    fetched.wait()
    block_a.step(0)
    swap(3, *swaps[3]).wait_recv()
    per_quarter = quarter // step

    @pl.loop(0, half // step)
    def _(i):
        b, inside = i // per_quarter, pl.ds(pl.multiple_of((i % per_quarter) * step, step), step)
        rows = pl.ds(pl.multiple_of(i * step, step), step)
        grad_in, gain_sum, shift_sum = norm_rows_back(
            stage[b, inside, :].astype(F32), acc[rows, :] + fold_in[0, rows, :].astype(F32), norm_ref[0:1, :]
        )
        sums[0, 0:1, :] += gain_sum
        sums[0, 1:2, :] += shift_sum
        send_rows[b, inside, :] = (x2[rows, :] + grad_in).astype(BF16)

    cell_gx = FromCell(here, send_rows, gx_ref, cell_sems[2], cell_sems[3])
    cell_gx.start()
    peers = (
        here.partner, here.over_x, here.over_y, {"dp": here.d, "mp": here.m + 1 - 2 * here.b},
        {"dp": here.d, "mp": here.m + 2 - 4 * here.t},
    )
    sum_send, sum_got = sems[-2:]

    def share(k):
        return remote(sums.at[k], sums_in.at[k], sum_send.at[k], sum_got.at[k], peers[k])

    def add_sums(k):
        share(k).wait_recv()
        sums[k + 1] = sums[k] + sums_in[k]
        if k < 4:
            share(k + 1).start()

    share(0).start()
    add_sums(0)
    add_sums(1)
    block_a.step(1)
    add_sums(2)
    block_1.finish(total, sum_1, total_sem)
    add_sums(3)
    block_a.step(2)
    add_sums(4)
    norm_out[...] = sums[5]
    block_a.step(3)
    block_a.step(4)
    block_a.step(5)
    for k in range(5):
        share(k).wait_send()
    cell_gx.arrive()
    block_a.finish(total, sum_a, total_sem)
    for role in range(2):
        for j in range(4):
            block_a.z_sent(role, j)
    cell_gx.sent()
    for n in (2, 3):
        swap(n, *swaps[n]).wait_send()


def backward(kept, heads, collective):
    kept, (norms, count) = kept[:14], kept[14:]
    (full_a, full_1, full_2, h1, qkv, ctx, lse, x_in, x2, h2, act, slope, gy, grad_2) = kept
    half, width = x2.shape
    quarter, seq = half // 2, 2 * half
    wide = act.shape[2]
    rows = width // 8
    inner = heads * HEAD_DIM
    dma = pltpu.SemaphoreType.DMA
    buffers = [
        (full_a.shape, BF16), (gy.shape, BF16), (slope.shape, BF16), (act.shape, BF16), (h2.shape, BF16), (x2.shape, F32),
        ((half, width), BF16), ((2, half, width), BF16), (ctx.shape, BF16), (ctx.shape, BF16), (lse.shape, F32),
        ((half, width), F32), (x_in.shape, BF16),
    ]
    own, part, landing, reduce_sems = Reduce.scratch(rows, wide)
    return pl.pallas_call(
        functools.partial(backward_kernel, heads),
        out_shape=[jax.ShapeDtypeStruct(x_in.shape, BF16)] * 2
        + [jax.ShapeDtypeStruct((rows, wide), F32)] * 3
        + [jax.ShapeDtypeStruct((4, width), F32)]
        + [jax.ShapeDtypeStruct(grad_2.shape, BF16)] * 2,
        in_specs=[VMEM] * 2 + [ANY] * 14,
        out_specs=[ANY] * 5 + [VMEM] + [ANY] * 2,
        scratch_shapes=[pltpu.VMEM(*s) for s in buffers]
        + [own, part] + landing * 3
        + [pltpu.VMEM((6, 4, width), F32), pltpu.VMEM((5, 4, width), F32)]
        + [dma] * 10 + [dma((4,)), dma((4,))] + [dma((2,))] * 4 + [dma((2,)), dma((2, 2)), dma]
        + reduce_sems * 3 + [dma((5,))] * 2,
        compiler_params=pltpu.CompilerParams(
            collective_id=collective, has_side_effects=True, vmem_limit_bytes=67043328
        ),
        name="backward",
    )(norms, count, *kept)


def gather_norms(routes, norm_params, d, m):
    cur = norm_params
    for bit in range(routes.mp_bits):
        got = routes.mp_bit(cur, bit)
        high = ((m >> bit) & 1) == 1
        cur = jnp.where(high, jnp.concatenate([got, cur], 1), jnp.concatenate([cur, got], 1))
    for bit in range(routes.bits + 1):
        got = routes.partner(cur) if bit == 0 else routes.pair_bit(cur, bit - 1)
        high = ((d >> bit) & 1) == 1
        cur = jnp.where(high, jnp.concatenate([got, cur], 1), jnp.concatenate([cur, got], 1))
    return cur


def scatter_norms(routes, grads, d, m):
    cur = grads
    for bit in reversed(range(routes.bits + 1)):
        low, up = jnp.split(cur, 2, axis=1)
        high = ((d >> bit) & 1) == 1
        give = jnp.where(high, low, up)
        got = routes.partner(give) if bit == 0 else routes.pair_bit(give, bit - 1)
        cur = jnp.where(high, up, low) + got
    for bit in reversed(range(routes.mp_bits)):
        low, up = jnp.split(cur, 2, axis=1)
        high = ((m >> bit) & 1) == 1
        cur = jnp.where(high, up, low) + routes.mp_bit(jnp.where(high, low, up), bit)
    return cur


def update(
    outputs, input_grad, norm_sum, attend_sum, expand_sum, reduce_sum, step_count, norm_params, norm_first, norm_second,
    attend_weight, attend_first, attend_second, output_weight, output_first, output_second,
    expand_weight, expand_first, expand_second, reduce_weight, reduce_first, reduce_second,
):
    width = attend_weight.shape[2]
    step_number = step_count[0].astype(F32)
    norm_new = adam_step(norm_params, norm_first, norm_second, norm_sum, norm_rate, 0.0, step_number)
    attend_reduced = jnp.stack([attend_sum[:, i * width : (i + 1) * width] for i in range(1, 4)])
    attend_new = adam_step(
        attend_weight, attend_first, attend_second, attend_reduced, 2.0 * D ** (-0.5), decay_rate, step_number
    )
    output_new = adam_step(
        output_weight, output_first, output_second, attend_sum[:, :width].T,
        2.0 * (2 * D // SEQ) ** (-0.5), decay_rate, step_number,
    )
    expand_new = adam_step(
        expand_weight, expand_first, expand_second, expand_sum, 2.0 * D ** (-0.5), decay_rate, step_number
    )
    reduce_new = adam_step(
        reduce_weight, reduce_first, reduce_second, reduce_sum.T, 2.0 * FF ** (-0.5), decay_rate, step_number
    )
    return (
        outputs, input_grad,
        norm_new[0], norm_new[1], norm_new[2][0:2], norm_new[2][2:4],
        *attend_new, *output_new, *expand_new, *reduce_new,
    )


def per_device_plain(
    inputs, cotangent, gene_counts, step_count, norm_params, norm_first, norm_second,
    attend_weight, attend_first, attend_second, output_weight, output_first, output_second,
    expand_weight, expand_first, expand_second, reduce_weight, reduce_first, reduce_second,
):
    routes = Routes(lax.axis_size("dp"), lax.axis_size("mp"))
    d, m = lax.axis_index("dp"), lax.axis_index("mp")
    c = d % 2
    cells, quarter, _ = inputs.shape
    assert routes.mp == 4 and 2 * cells == routes.mp and routes.dp % 2 == 0
    half = 2 * quarter
    seq = 2 * half
    heads = attend_weight.shape[2] // HEAD_DIM
    width = heads * HEAD_DIM
    m_low, m_high = m % 2, m // 2
    mask = 2 * (d // 2) + ((c + m_high) % 2)

    norm_full = gather_norms(routes, norm_params, d, m)

    def to_cell(values):
        got = [
            routes.cell(lax.dynamic_index_in_dim(values, (m_low + k) % 2, 0, keepdims=False), k) for k in range(2)
        ]
        return jnp.concatenate(got, 0)

    def from_cell(rows):
        rows = rows.astype(BF16)
        got = [routes.cell(rows[k * quarter : (k + 1) * quarter], k, back=True) for k in range(2)]
        flip = m_low == 1
        return jnp.stack([jnp.where(flip, got[1], got[0]), jnp.where(flip, got[0], got[1])]).astype(F32)

    attend_shard = jnp.concatenate(
        [output_weight.T, attend_weight[0], attend_weight[1], attend_weight[2]], axis=1
    ).astype(BF16)
    expand_shard = expand_weight.astype(BF16)
    reduce_shard = reduce_weight.T.astype(BF16)

    x_mine = to_cell(inputs).astype(F32)
    attend_w = [assemble(pieces, mask) for pieces in gather_shards(routes, attend_shard)]
    expand_w = [assemble(pieces, mask) for pieces in gather_shards(routes, expand_shard)]
    reduce_w = [assemble(pieces, mask) for pieces in gather_shards(routes, reduce_shard)]
    gy_mine = to_cell(cotangent)

    other_counts = routes.partner(gene_counts)
    mine = jnp.where(m_high == c, gene_counts, other_counts)
    count = jnp.where(m_low == 1, mine[1], mine[0])
    inside = jnp.arange(quarter)
    first = m_low
    positions = jnp.concatenate(
        [h * half + b * quarter + inside for h, b in ((c, first), (c, 1 - first), (1 - c, first), (1 - c, 1 - first))]
    )
    bias = jnp.where(positions < 1 + count, 0.0, masked_score).astype(F32)

    def both(rows):
        return jnp.concatenate([rows, routes.partner(rows)], 0)

    def fold(partial):
        return partial[:half] + routes.partner(partial[half:].astype(BF16)).astype(F32)

    normed, scaled_one, inv_one = normalize(x_mine, norm_full[0], norm_full[1])
    h1 = both(normed.astype(BF16))
    qkv = jnp.stack([mm_nn(h1, w[:, width:]).astype(BF16) for w in attend_w])
    ctx, lse = attend(qkv, bias[None, :], heads)
    branch = mm_nt(ctx[0], attend_w[0][:, :width]) + mm_nt(ctx[1], attend_w[1][:, :width])
    x2 = x_mine + fold(branch)
    normed, scaled_two, inv_two = normalize(x2, norm_full[2], norm_full[3])
    h2 = both(normed.astype(BF16))
    hidden = [mm_nn(h2, w) for w in expand_w]
    active = [exact_gelu(u).astype(BF16) for u in hidden]
    branch = mm_nt(active[0], reduce_w[0]) + mm_nt(active[1], reduce_w[1])
    outputs = from_cell(x2 + fold(branch))

    gy = both(gy_mine)
    reduce_grad = [mm_tn(gy, a).astype(BF16) for a in active]
    grad_hidden = [
        jax.vjp(exact_gelu, u)[1](mm_nn(gy, w))[0].astype(BF16) for u, w in zip(hidden, reduce_w)
    ]
    expand_grad = [mm_tn(h2, g).astype(BF16) for g in grad_hidden]
    gh2 = fold(mm_nt(grad_hidden[0], expand_w[0]) + mm_nt(grad_hidden[1], expand_w[1]))
    grad_in, gain_two, shift_two = normalize_back(gh2, scaled_two, inv_two, norm_full[2])
    gx2 = gy_mine.astype(F32) + grad_in
    gb = both(gx2.astype(BF16))
    grad_ctx = jnp.stack([mm_nn(gb, w[:, :width]).astype(BF16) for w in attend_w])
    gq, gkv = attend_back(qkv, grad_ctx, ctx, lse, bias[:, None], heads)
    attend_grad = [
        jnp.concatenate(
            [mm_tn(gb, ctx[i]), mm_tn(h1, gq[i]), mm_tn(h1, gkv[i])], axis=1
        ).astype(BF16)
        for i in range(2)
    ]
    gh1 = fold(
        sum(
            mm_nt(gq[i], attend_w[i][:, width : 2 * width]) + mm_nt(gkv[i], attend_w[i][:, 2 * width :])
            for i in range(2)
        )
    )
    grad_in, gain_one, shift_one = normalize_back(gh1, scaled_one, inv_one, norm_full[0])
    input_grad = from_cell(gx2 + grad_in)

    reduce_sum = scatter_grads(routes, reduce_grad, mask)
    expand_sum = scatter_grads(routes, expand_grad, mask)
    attend_sum = scatter_grads(routes, attend_grad, mask)
    norm_sum = scatter_norms(routes, jnp.stack([gain_one, shift_one, gain_two, shift_two]), d, m)

    return update(
        outputs, input_grad, norm_sum, attend_sum, expand_sum, reduce_sum, step_count, norm_params, norm_first,
        norm_second, attend_weight, attend_first, attend_second, output_weight, output_first, output_second,
        expand_weight, expand_first, expand_second, reduce_weight, reduce_first, reduce_second,
    )


def per_device(
    inputs, cotangent, gene_counts, step_count, norm_params, norm_first, norm_second,
    attend_weight, attend_first, attend_second, output_weight, output_first, output_second,
    expand_weight, expand_first, expand_second, reduce_weight, reduce_first, reduce_second,
):
    d, m, mp_size = lax.axis_index("dp"), lax.axis_index("mp"), lax.axis_size("mp")
    cells = inputs.shape[0]
    assert mp_size == 4 and 2 * cells == mp_size and lax.axis_size("dp") == 8
    heads = attend_weight.shape[2] // HEAD_DIM
    shards = (
        jnp.concatenate([output_weight.T, attend_weight[0], attend_weight[1], attend_weight[2]], axis=1).astype(BF16),
        expand_weight.astype(BF16),
        reduce_weight.T.astype(BF16),
    )
    slot = jnp.zeros((8, 128), F32)
    slot = slot.at[0:4, 0 : norm_params.shape[1]].set(norm_params).at[4, 0:cells].set(gene_counts.astype(F32))
    kept = forward(inputs, cotangent, shards, slot, heads, 1)
    outputs, input_grad, attend_sum, expand_sum, reduce_sum, norm_part, _, _ = backward(kept, heads, 2)
    outputs, input_grad = outputs.astype(F32), input_grad.astype(F32)
    columns = norm_params.shape[1]
    norm_sum = lax.dynamic_slice(norm_part, (0, (d * mp_size + m) * columns), (4, columns))
    return update(
        outputs, input_grad, norm_sum, attend_sum, expand_sum, reduce_sum, step_count, norm_params, norm_first,
        norm_second, attend_weight, attend_first, attend_second, output_weight, output_first, output_second,
        expand_weight, expand_first, expand_second, reduce_weight, reduce_first, reduce_second,
    )


def solution(mesh):
    norms = P(None, ("dp", "mp"))
    attend_spec, col, row = P(None, "dp", "mp"), P("mp", "dp"), P("dp", "mp")
    tokens = P("dp", "mp", None)
    return jax.shard_map(
        per_device if mesh.shape["dp"] == 8 else per_device_plain,
        mesh=mesh,
        in_specs=(tokens, tokens, P("dp"), P(), norms, norms, norms)
        + (attend_spec,) * 3 + (col,) * 3 + (row,) * 3 + (col,) * 3,
        out_specs=(tokens, tokens, norms, norms, norms, norms)
        + (attend_spec,) * 3 + (col,) * 3 + (row,) * 3 + (col,) * 3,
        check_vma=False,
    )
```

profile of v0, /device:TPU:1, one launch (start us, length us, event | category | flops | bytes accessed | tf_op | source)
XLA Modules:
  0.0 444.6 jit_solution(16040120277569141202)
XLA Ops:
  0.7 1.3 convert.16
  2.0 1.0 convert_bitcast_fusion.1
  3.0 1.0 concatenate.8.refs_2_
  4.0 0.8 convert_bitcast_fusion.refs_4_
  4.8 0.8 convert_element_type.22.refs_3_
  5.6 0.6 scatter.6
  6.2 1.3 scatter.9.refs_5_
  7.5 203.4 %forward.1 = (bf16[2,1280,1280]{2,1,0:T(8,128)(2,1)}, bf16[2,1280,1280]{2,1,0:T(8,128)(2,1)}, bf16[2,1280,1280]{2,1,0:T(8,128)(2,1)}, bf16[1024,1280]{1,0:T(8,12...) custom-call(bf16[2,256,1280]{2,1,0:T(8,128)(2,1)} %refs_0_.1, ...), custom_call_target="tpu_custom_call" | custom-call | tf_op jit(solution)/shard_map/forward/pallas_call | solution.py:796
  210.8 215.2 %backward.1 = (bf16[2,256,1280]{2,1,0:T(8,128)(2,1)}, bf16[2,256,1280]{2,1,0:T(8,128)(2,1)}, f32[160,1280]{1,0:T(8,128)}, f32[160,1280]{1,0:T(8,128)}, f32[160,1...) custom-call(f32[4,1280]{1,0:T(4,128)} %get-tuple-element.64.refs_0_, ...), custom_call_target="tpu_custom_call" | custom-call | tf_op jit(solution)/shard_map/backward/pallas_call | solution.py:1320
  426.1 1.4 slice_bitcast_fusion.2
  428.3 3.3 multiply_subtract_fusion.2
  431.5 1.7 convert_element_type.26
  433.2 0.1 copy-done.4
  433.3 1.7 convert_element_type.27
  435.1 0.7 copy-done.8
  435.8 0.2 copy-done.12
  436.1 1.8 multiply_subtract_fusion
  437.9 0.1 copy-done.9
  438.0 0.6 copy-done.10
  438.6 0.2 copy-done.11
  438.9 1.8 multiply_subtract_fusion.1
  440.7 1.9 multiply_subtract_fusion.3
  442.6 1.4 multiply_subtract_fusion.4
  444.0 0.6 fusion.14
  (36 shorter events, 0.2 us)
Async XLA Ops:
  0.7 3.3 copy-start
  0.7 4.1 copy-start.2
  0.7 4.9 %copy-start.15 = (f32[4,40]{1,0:T(4,128)S(1)}, f32[4,40]{1,0:T(4,128)}, u32[]{:S(2)}) copy-start(f32[4,40]{1,0:T(4,128)} %param.27) | copy-start | bytes 1924
  0.7 5.5 %copy-start.19 = (s32[2]{0:T(128)S(1)}, s32[2]{0:T(128)}, u32[]{:S(2)}) copy-start(s32[2]{0:T(128)} %param.25) | copy-start | bytes 28
  427.4 4.1 copy-start.5
  431.5 1.8 copy-start.4
  433.2 1.8 copy-start.1
  433.2 1.9 copy-start.7
  433.2 2.6 copy-start.8
  433.2 2.8 copy-start.12
  436.1 1.8 copy-start.3
  436.1 1.9 copy-start.9
  436.1 2.5 copy-start.10
  436.1 2.8 copy-start.11
  438.8 1.9 copy-start.6
  438.8 1.9 copy-start.13
  438.8 1.9 copy-start.14
  438.9 3.8 copy-start.16
  438.9 3.8 copy-start.17
  438.9 3.8 copy-start.18
where the time goes:
time: 445 us
  Pallas kernels  419 us (94%)
  other arithmetic  17.4 us (4%)
  local copies, waits for them, and re-layouts  7.01 us (2%)
    pallas_call x1, Pallas kernels, backward(): pl.pallas_call(functools.partial(backward_kernel, heads), out_shape=[jax....  215 us
    pallas_call x1, Pallas kernels, forward(): pl.pallas_call(functools.partial(forward_kernel, heads), out_shape=[jax.S...  203 us
    sub x5, other arithmetic, adam_step(): return (weight - rate * (update + decay * weight), first_new, second_new)  10.2 us

commit v1 on v0

--- a/solution.py
+++ b/solution.py
@@ -589,7 +589,7 @@
     per = len(Gather.scratch())
     norms = Norms(here, slot_ref, slots, sems[9 + 3 * per :])
     block_a, block_1, block_2 = (
-        Gather(here, shard, full, sems[9 + per * i : 9 + per * (i + 1)], i == 0)
+        Gather(here, shard, full, sems[9 + per * i : 9 + per * (i + 1)], i <= 1)
         for i, (shard, full) in enumerate(((shard_a, full_a), (shard_1, full_1), (shard_2, full_2)))
     )
     cell_x = ToCell(here, x_ref, x_in, cell_sems[0], cell_sems[1])
@@ -649,6 +649,8 @@
     swap_h1.start()
     stores.put(x_in, x_out)
     pl.when(away)(lambda: block_1.spread(0))
+    block_1.spread(1)
+    block_2.start_far()
     block_a.arrive()
     pl.when(here.home)(lambda: block_1.relay(0))
     pl.when(here.home)(lambda: block_2.spread(0))
@@ -670,11 +672,11 @@
 
     @pl.loop(0, 2 * per_chunk)
     def _(i):
-        pl.when(jnp.logical_and(i == 1, away))(lambda: block_1.relay(0))
-        pl.when(i == 4)(lambda: block_1.spread(1))
-        pl.when(i == 4)(lambda: block_2.start_far())
-        pl.when(jnp.logical_and(i == 5, here.home))(lambda: block_2.relay(0))
-        pl.when(i == 7)(lambda: block_1.relay(1))
+        pl.when(jnp.logical_and(i == 0, away))(lambda: block_1.relay(0))
+        pl.when(i == 3)(lambda: block_1.relay(1))
+        pl.when(jnp.logical_and(i == 4, here.home))(lambda: block_2.relay(0))
+        pl.when(jnp.logical_and(i == 5, away))(lambda: block_2.spread(0))
+        pl.when(i == 7)(lambda: block_2.spread(1))
         attend_rows(
             bias, qkv, ctx, lse, i // per_chunk, pl.multiple_of((i % per_chunk) * q_block, q_block), q_block, heads
         )
@@ -701,7 +703,6 @@
             rows = pl.ds(b * quarter, quarter)
             x2[rows, cols] = x_in[b, :, cols].astype(F32) + part[b * quarter : (b + 1) * quarter]
 
-    pl.when(away)(lambda: block_2.spread(0))
     swap_fold.wait_recv()
 
     @pl.loop(0, half // step)
@@ -724,8 +725,7 @@
     @pl.loop(0, 2 * per_unit)
     def _(i):
         pl.when(jnp.logical_and(i == 0, away))(lambda: block_2.relay(0))
-        pl.when(i == 3)(lambda: block_2.spread(1))
-        pl.when(i == 9)(lambda: block_2.relay(1))
+        pl.when(i == 5)(lambda: block_2.relay(1))
         b, cols = i // per_unit, pl.ds(pl.multiple_of((i % per_unit) * 256, 256), 256)
         value, grad = exact_gelu_both(mm_nn(h2[...], weight[b, :, cols]))
         act[b, :, cols] = value.astype(BF16)
@@ -893,8 +893,7 @@
         for n in range(2):
             self.load_piece(role, n, j).wait()
             arrived(self.one.at[role, n, j], self.got_one.at[role, n, j], h.over_x)
-            total = self.own[role, n].astype(F32) + self.one[role, n, j].astype(F32)
-            self.one[role, n, j] = total.astype(BF16)
+            self.one[role, n, j] = self.own[role, n] + self.one[role, n, j]
             if n == 0:
                 self.copy_two(role, j).start()
             if j < 3:
@@ -902,7 +901,7 @@
 
     def add_two(self, role, j):
         arrived(self.two.at[role, j], self.got_two.at[role, j], self.here.over_x)
-        total = (self.one[role, 1, j].astype(F32) + self.two[role, j].astype(F32)).astype(BF16)
+        total = self.one[role, 1, j] + self.two[role, j]
         if self.before is not None:
             self.before.z_sent(role, j)
 
@@ -921,8 +920,7 @@
         @pl.when(jnp.logical_and(self.away, jnp.logical_not(self.outer)))
         def _():
             arrived(self.far.at[role, j], self.got_far.at[role, j], self.here.partner)
-            total = self.part[role, j].astype(F32) + self.far[role, j].astype(F32)
-            self.part[role, j] = total.astype(BF16)
+            self.part[role, j] = self.part[role, j] + self.far[role, j]
             self.to_owner(role, j).start()
 
     def step(self, j):
@@ -1236,7 +1234,6 @@
         ).astype(BF16)
 
     swap(3, *swaps[3]).start()
-    block_2.finish(total, sum_2, total_sem)
     block_1.step(5)
 
     @pl.loop(0, tiles)
@@ -1278,18 +1275,19 @@
             share(k + 1).start()
 
     share(0).start()
+    block_a.step(1)
     add_sums(0)
+    block_2.finish(total, sum_2, total_sem)
+    block_a.step(2)
     add_sums(1)
-    block_a.step(1)
+    block_a.step(3)
     add_sums(2)
     block_1.finish(total, sum_1, total_sem)
+    block_a.step(4)
     add_sums(3)
-    block_a.step(2)
+    block_a.step(5)
     add_sums(4)
     norm_out[...] = sums[5]
-    block_a.step(3)
-    block_a.step(4)
-    block_a.step(5)
     for k in range(5):
         share(k).wait_send()
     cell_gx.arrive()

time: 445 us -> 432 us (0.971)
  Pallas kernels: 419 us -> 404 us
    pallas_call x1, Pallas kernels: 203 us -> 193 us  [forward(): pl.pallas_call(functools.partial(forward_kernel, heads), out_shape=[jax.S...]
where the time goes in v1:
time: 432 us; the launch traced here: 430 us
  Pallas kernels  404 us (94%)
  other arithmetic  17.4 us (4%)
  local copies, waits for them, and re-layouts  7.01 us (2%)
    pallas_call x1, Pallas kernels, backward(): pl.pallas_call(functools.partial(backward_kernel, heads), out_shape=[jax....  211 us
    pallas_call x1, Pallas kernels, forward(): pl.pallas_call(functools.partial(forward_kernel, heads), out_shape=[jax.S...  193 us
    sub x5, other arithmetic, adam_step(): return (weight - rate * (update + decay * weight), first_new, second_new)  10.2 us

profile of v1, /device:TPU:1, one launch (start us, length us, event | category | flops | bytes accessed | tf_op | source)
XLA Modules:
  0.0 429.9 jit_solution(11643984527632131997)
XLA Ops:
  0.7 1.3 convert.16
  2.0 1.0 convert_bitcast_fusion.1
  3.0 1.0 concatenate.8.refs_2_
  4.0 0.8 convert_bitcast_fusion.refs_4_
  4.8 0.8 convert_element_type.22.refs_3_
  5.6 0.6 scatter.6
  6.2 1.3 scatter.9.refs_5_
  7.5 192.6 %forward.1 = (bf16[2,1280,1280]{2,1,0:T(8,128)(2,1)}, bf16[2,1280,1280]{2,1,0:T(8,128)(2,1)}, bf16[2,1280,1280]{2,1,0:T(8,128)(2,1)}, bf16[1024,1280]{1,0:T(8,12...) custom-call(bf16[2,256,1280]{2,1,0:T(8,128)(2,1)} %refs_0_.1, ...), custom_call_target="tpu_custom_call" | custom-call | tf_op jit(solution)/shard_map/forward/pallas_call | solution.py:796
  200.1 211.3 %backward.1 = (bf16[2,256,1280]{2,1,0:T(8,128)(2,1)}, bf16[2,256,1280]{2,1,0:T(8,128)(2,1)}, f32[160,1280]{1,0:T(8,128)}, f32[160,1280]{1,0:T(8,128)}, f32[160,1...) custom-call(f32[4,1280]{1,0:T(4,128)} %get-tuple-element.64.refs_0_, ...), custom_call_target="tpu_custom_call" | custom-call | tf_op jit(solution)/shard_map/backward/pallas_call | solution.py:1318
  411.4 1.4 slice_bitcast_fusion.2
  413.6 3.3 multiply_subtract_fusion.2
  416.9 1.7 convert_element_type.26
  418.6 0.1 copy-done.4
  418.7 1.7 convert_element_type.27
  420.4 0.7 copy-done.8
  421.2 0.2 copy-done.12
  421.4 1.8 multiply_subtract_fusion
  423.2 0.1 copy-done.9
  423.4 0.6 copy-done.10
  423.9 0.2 copy-done.11
  424.2 1.8 multiply_subtract_fusion.1
  426.1 1.9 multiply_subtract_fusion.3
  428.0 1.4 multiply_subtract_fusion.4
  429.3 0.6 fusion.14
  (36 shorter events, 0.2 us)
Async XLA Ops:
  0.7 3.3 copy-start
  0.7 4.1 copy-start.2
  0.7 4.9 %copy-start.15 = (f32[4,40]{1,0:T(4,128)S(1)}, f32[4,40]{1,0:T(4,128)}, u32[]{:S(2)}) copy-start(f32[4,40]{1,0:T(4,128)} %param.27) | copy-start | bytes 1924
  0.7 5.5 %copy-start.19 = (s32[2]{0:T(128)S(1)}, s32[2]{0:T(128)}, u32[]{:S(2)}) copy-start(s32[2]{0:T(128)} %param.25) | copy-start | bytes 28
  412.8 4.1 copy-start.5
  416.9 1.8 copy-start.4
  418.6 1.8 copy-start.1
  418.6 1.9 copy-start.7
  418.6 2.6 copy-start.8
  418.6 2.8 copy-start.12
  421.4 1.8 copy-start.3
  421.4 1.9 copy-start.9
  421.4 2.5 copy-start.10
  421.4 2.8 copy-start.11
  424.2 1.9 copy-start.6
  424.2 1.9 copy-start.13
  424.2 1.9 copy-start.14
  424.2 3.8 copy-start.16
  424.2 3.8 copy-start.17
  424.2 3.8 copy-start.18

commit v2 on v1

--- a/solution.py
+++ b/solution.py
@@ -620,11 +620,11 @@
     norms.start(1)
     cell_x.start()
     block_a.spread(1)
+    block_1.start_far()
     norms.wait(1)
     norms.start(2)
     block_a.relay(1)
     pl.when(here.home)(lambda: block_1.spread(0))
-    block_1.start_far()
     norms.wait(2)
     columns = norm_ref.shape[1] // 32
     for n in range(32):

time: 432 us -> 421 us (0.975)
  Pallas kernels: 404 us -> 394 us
    pallas_call x1, Pallas kernels: 193 us -> 186 us  [forward(): pl.pallas_call(functools.partial(forward_kernel, heads), out_shape=[jax.S...]
where the time goes in v2:
time: 421 us; the launch traced here: 420 us
  Pallas kernels  394 us (94%)
  other arithmetic  17.4 us (4%)
  local copies, waits for them, and re-layouts  7.01 us (2%)
    pallas_call x1, Pallas kernels, backward(): pl.pallas_call(functools.partial(backward_kernel, heads), out_shape=[jax....  208 us
    pallas_call x1, Pallas kernels, forward(): pl.pallas_call(functools.partial(forward_kernel, heads), out_shape=[jax.S...  186 us
    sub x5, other arithmetic, adam_step(): return (weight - rate * (update + decay * weight), first_new, second_new)  10.2 us

profile of v2, /device:TPU:1, one launch (start us, length us, event | category | flops | bytes accessed | tf_op | source)
XLA Modules:
  0.0 420.4 jit_solution(15313249682121822533)
XLA Ops:
  0.7 1.3 convert.16
  2.0 1.0 convert_bitcast_fusion.1
  3.0 1.0 concatenate.8.refs_2_
  4.0 0.8 convert_bitcast_fusion.refs_4_
  4.8 0.8 convert_element_type.22.refs_3_
  5.6 0.6 scatter.6
  6.2 1.3 scatter.9.refs_5_
  7.5 186.2 %forward.1 = (bf16[2,1280,1280]{2,1,0:T(8,128)(2,1)}, bf16[2,1280,1280]{2,1,0:T(8,128)(2,1)}, bf16[2,1280,1280]{2,1,0:T(8,128)(2,1)}, bf16[1024,1280]{1,0:T(8,12...) custom-call(bf16[2,256,1280]{2,1,0:T(8,128)(2,1)} %refs_0_.1, ...), custom_call_target="tpu_custom_call" | custom-call | tf_op jit(solution)/shard_map/forward/pallas_call | solution.py:796
  193.7 208.2 %backward.1 = (bf16[2,256,1280]{2,1,0:T(8,128)(2,1)}, bf16[2,256,1280]{2,1,0:T(8,128)(2,1)}, f32[160,1280]{1,0:T(8,128)}, f32[160,1280]{1,0:T(8,128)}, f32[160,1...) custom-call(f32[4,1280]{1,0:T(4,128)} %get-tuple-element.64.refs_0_, ...), custom_call_target="tpu_custom_call" | custom-call | tf_op jit(solution)/shard_map/backward/pallas_call | solution.py:1318
  401.8 1.4 slice_bitcast_fusion.2
  404.1 3.3 multiply_subtract_fusion.2
  407.3 1.7 convert_element_type.26
  409.0 0.1 copy-done.4
  409.1 1.7 convert_element_type.27
  410.9 0.7 copy-done.8
  411.6 0.2 copy-done.12
  411.9 1.8 multiply_subtract_fusion
  413.7 0.1 copy-done.9
  413.8 0.6 copy-done.10
  414.4 0.2 copy-done.11
  414.7 1.8 multiply_subtract_fusion.1
  416.5 1.9 multiply_subtract_fusion.3
  418.4 1.4 multiply_subtract_fusion.4
  419.8 0.6 fusion.14
  (36 shorter events, 0.2 us)
Async XLA Ops:
  0.7 3.3 copy-start
  0.7 4.1 copy-start.2
  0.7 4.9 %copy-start.15 = (f32[4,40]{1,0:T(4,128)S(1)}, f32[4,40]{1,0:T(4,128)}, u32[]{:S(2)}) copy-start(f32[4,40]{1,0:T(4,128)} %param.27) | copy-start | bytes 1924
  0.7 5.5 %copy-start.19 = (s32[2]{0:T(128)S(1)}, s32[2]{0:T(128)}, u32[]{:S(2)}) copy-start(s32[2]{0:T(128)} %param.25) | copy-start | bytes 28
  403.2 4.1 copy-start.5
  407.3 1.8 copy-start.4
  409.0 1.8 copy-start.1
  409.0 1.9 copy-start.7
  409.0 2.6 copy-start.8
  409.0 2.8 copy-start.12
  411.9 1.8 copy-start.3
  411.9 1.9 copy-start.9
  411.9 2.5 copy-start.10
  411.9 2.8 copy-start.11
  414.6 1.9 copy-start.6
  414.6 1.9 copy-start.13
  414.6 1.9 copy-start.14
  414.6 3.8 copy-start.16
  414.6 3.8 copy-start.17
  414.7 3.8 copy-start.18
